TPU v7x, 256 devices: a whole 4x4x8 slice. The times are simulated.
256 devices in a mesh: layer: 32 (over y, z), xs: 8 (over x, core).
Axes of the slice: x: 4, y: 4, z: 8, core: 2. Of those that a mesh axis runs over, the one named last changes fastest.
Arguments:
- probes: float32 [64, 32, 16, 640], P('layer', None, 'xs'), may hold values from -6 to 6
- potential: float32 [64, 16, 640], P('layer', 'xs'), may hold values from -1 to 1
- projector: bfloat16 [64, 512, 1280], P('layer', 'xs'), may hold values from -0.15625 to 0.15625
- intersection_ids: int32 [64, 512], P('layer', 'xs'), may hold values from 0 to 255
- strength: float32 [64, 256], P('layer'), may hold values from -2 to 2
- decay_rates: float32 [64, 32], P('layer'), may hold values from 0.3 to 1
- contour_nodes: float32 [4], replicated, may hold values from -1 to 3
- node_weights: float32 [4], replicated, may hold values from 0.5 to 1.5
Outputs:
- moments: float32 [2, 64, 32, 16, 640], P(None, 'layer', None, 'xs')
All inputs are finite; a program needn't handle non-finite values.
Results may differ from a plain program's by a relative error of at most 0.00059.
Values sent between devices are 32-bit elements; how exact they have to be, the bound alone decides.
A program may use at most 64 MiB of HBM per device.

v0:
```python
import jax
import jax.numpy as jnp
from jax import lax
from jax.sharding import PartitionSpec as P

NPROJ = 256
FAR = -1.0 / 12.0
NEAR = 4.0 / 3.0
CENTER = -2.5


def carried_in(part, axis, combine, identity, reverse):
    count = lax.axis_size(axis)
    place = lax.axis_index(axis)
    ahead = count - 1 - place if reverse else place
    gathered = jax.tree.map(lambda a: lax.all_gather(a, axis), part)
    state = jax.tree.map(lambda a, e: jnp.zeros_like(a) + jnp.asarray(e, a.dtype), part, identity)

    def one(lap, state):
        source = count - 1 - lap if reverse else lap
        return combine(
            state, jax.tree.map(lambda a: lax.dynamic_index_in_dim(a, source, 0, False), gathered)
        )

    return lax.fori_loop(0, ahead, one, state)


def with_halo(cells, sides, width):
    for axis, dim in sides:
        count = lax.axis_size(axis)
        ends = count - 1
        head = lax.slice_in_dim(cells, 0, width, axis=dim)
        tail = lax.slice_in_dim(cells, cells.shape[dim] - width, cells.shape[dim], axis=dim)
        cells = jnp.concatenate(
            [
                lax.ppermute(tail, axis, [(i, (i + 1) % count) for i in range(ends)]),
                cells,
                lax.ppermute(head, axis, [((i + 1) % count, i) for i in range(ends)]),
            ],
            axis=dim,
        )
    return cells


def second_along(padded, axis, count):

    def piece(offset):
        return lax.slice_in_dim(padded, 2 + offset, 2 + offset + count, axis=axis)

    return FAR * (piece(-2) + piece(2)) + NEAR * (piece(-1) + piece(1)) + CENTER * piece(0)


def combine(earlier, later):
    return (earlier[0] * later[0], later[0][:, None, None] * earlier[1] + later[1])


def scan_sweeps(forcing, decay_rates):
    count = forcing.shape[1]
    zero = jnp.zeros_like(forcing[:, 0])
    through = jnp.prod(decay_rates, axis=0)
    state = zero
    ahead_list = []
    for index in range(count):
        rate = decay_rates[index][:, None, None]
        state = rate * state + (1.0 - rate) * forcing[:, index]
        ahead_list.append(state)
    ahead_zero = jnp.stack(ahead_list, axis=1)
    entering = carried_in(
        (through, ahead_zero[:, -1]), "layer", combine, (jnp.ones_like(through), zero), False
    )[1]
    lower_prod = jnp.cumprod(decay_rates, axis=0)
    ahead = ahead_zero + lower_prod[None, :, :, None, None] * entering[:, None]
    state = zero
    back_list = []
    for index in reversed(range(count)):
        rate = decay_rates[index][:, None, None]
        state = rate * state + (1.0 - rate) * ahead[:, index]
        back_list.append(state)
    back_zero = jnp.stack(back_list[::-1], axis=1)
    from_above = carried_in(
        (through, back_zero[:, 0]), "layer", combine, (jnp.ones_like(through), zero), True
    )[1]
    upper_prod = jnp.cumprod(decay_rates[::-1], axis=0)[::-1]
    return back_zero + upper_prod[None, :, :, None, None] * from_above[:, None]


def run_sweeps(forcing, decay_rates):
    return scan_sweeps(forcing, decay_rates)


def shards(
    probes,
    potential,
    projector,
    intersection_ids,
    strength,
    decay_rates,
    contour_nodes,
    node_weights,
):
    layers, columns, rows, depth = probes.shape
    padded = with_halo(probes, (("layer", 0), ("xs", 2)), 2)
    across = jnp.pad(probes, ((0, 0), (0, 0), (0, 0), (2, 2)))
    laplace = second_along(padded[:, :, 2:-2, :], 0, layers)
    laplace = laplace + second_along(padded[2:-2], 2, rows)
    laplace = laplace + second_along(across, 3, depth)
    rounded = probes.astype(jnp.bfloat16).reshape(layers, columns, rows * depth)
    slot_coef = jnp.einsum("lsp,lcp->lsc", projector, rounded, preferred_element_type=jnp.float32)
    onehot = (intersection_ids[:, :, None] == jnp.arange(NPROJ, dtype=jnp.int32)).astype(
        jnp.float32
    )
    partial_coef = jnp.einsum("lsq,lsc->lqc", onehot, slot_coef, precision=lax.Precision.HIGHEST)
    coef = lax.psum(partial_coef, "xs")
    scaled = (strength[:, :, None] * coef).astype(jnp.bfloat16)
    slot_back = jnp.einsum(
        "lsq,lqc->lsc", onehot.astype(jnp.bfloat16), scaled, preferred_element_type=jnp.float32
    ).astype(jnp.bfloat16)
    projected = jnp.einsum(
        "lsp,lsc->lcp", projector, slot_back, preferred_element_type=jnp.float32
    ).reshape(layers, columns, rows, depth)
    hamil = -0.5 * laplace + potential[:, None] * probes + projected
    forcing = hamil[None] - contour_nodes[:, None, None, None, None] * probes[None]
    swept = run_sweeps(forcing, decay_rates)
    first = jnp.sum(node_weights[:, None, None, None, None] * swept, axis=0)
    second = jnp.sum((node_weights * contour_nodes)[:, None, None, None, None] * swept, axis=0)
    return jnp.stack([first, second])


def solution(mesh):
    in_specs = (
        P("layer", None, "xs", None),
        P("layer", "xs", None),
        P("layer", "xs", None),
        P("layer", "xs"),
        P("layer", None),
        P("layer", None),
        P(),
        P(),
    )
    out_specs = P(None, "layer", None, "xs", None)
    return jax.shard_map(shards, mesh=mesh, in_specs=in_specs, out_specs=out_specs, check_vma=False)
```

profile of v0, /device:TPU:1, one launch (start us, length us, event | category | flops | bytes accessed | tf_op | source)
XLA Modules:
  0.0 558.4 jit_solution(769351655144849599)
XLA Ops:
  6.5 4.5 collective-permute-start
  11.1 1.3 collective-permute-start.1
  12.4 5.4 collective-permute-done
  17.8 2.0 constant_dynamic-update-slice_fusion.1
  19.8 2.0 collective-permute-done.1
  21.9 3.6 collective-permute-start.3
  25.5 3.0 collective-permute-start.2
  28.5 1.0 reshape.100
  31.5 62.9 %all-reduce.4.cloned.1.call-done = f32[2,256,32]{1,2,0:T(8,128)} async-done(((f32[2,256,32]{1,2,0:T(8,128)}), f32[2,256,32]{1,2,0:T(8,128)}) %all-reduce.4.cloned.1.call-update) | async-done | bytes 65552 | tf_op jit(solution)/shard_map/psum | solution.py:113
  94.4 1.9 fusion.2
  96.3 1.9 reshape.101
  98.2 3.2 add_add_fusion
  104.4 61.3 %all-reduce.1 = f32[1024]{0:T(1024)S(1)} all-reduce(f32[1024]{0:T(1024)S(1)} %dynamic-update-slice), channel_id=2, replica_groups=mesh['layer'=32,'xs'=8] {'layer'}, use_global_device_ids=true, to_apply=%add.1 | all-reduce | flops 1024 | bytes 8192
  166.0 99.1 %all-gather.4.cloned.1.call-done = f32[32,4,32,2,640]{4,2,3,1,0:T(8,128)} async-done(((f32[1,4,32,2,640]{4,2,3,1,0:T(8,128)}), f32[32,4,32,2,640]{4,2,3,1,0:T(8,128)}) %all-gather.4.cloned.1.call-update) | async-done | bytes 20971536 | tf_op jit(solution)/shard_map/all_gather | solution.py:16
  267.0 219.5 %all-gather.6.cloned.1.call-done = f32[32,4,32,2,640]{4,2,3,1,0:T(8,128)} async-done(((f32[1,4,32,2,640]{4,2,3,1,0:T(8,128)}), f32[32,4,32,2,640]{4,2,3,1,0:T(8,128)}) %all-gather.6.cloned.1.call-update) | async-done | bytes 20971536 | tf_op jit(solution)/shard_map/all_gather | solution.py:16
  486.7 63.4 %while.27 = (s32[]{:T(128)}, f32[4,32,2,640]{3,2,1,0:T(2,128)S(1)}, s32[]{:T(128)}, f32[32,32]{1,0:T(8,128)S(1)}, f32[32,4,32,2,640]{4,2,3,1,0:T(8,128)}, /*index=5*/s32[]{:T(128)}, s32[]{:T(128)}, s32[]{:T(128)}, s32[]{:T(128)}) while((s32[]{:T(128)}, f32[4,32,2,640]{3,2,1,0:T(2,128)S(1)}, s32[]{:T(128)}, f32[32,32]{1,0:T(8,128)S(1)}, ...), condition=%wide.region_7.8_spmd, body=%wide.region_6.7_spmd.sunk | while | flops 327686 | bytes 3277339 | solution.py:25
  486.7 1.1 constant_dynamic-slice_fusion.5
  488.7 1.1 constant_dynamic-slice_fusion.5
  490.8 1.1 constant_dynamic-slice_fusion.5
  492.8 1.1 constant_dynamic-slice_fusion.5
  494.9 1.1 constant_dynamic-slice_fusion.5
  496.9 1.1 constant_dynamic-slice_fusion.5
  499.0 1.1 constant_dynamic-slice_fusion.5
  501.0 1.1 constant_dynamic-slice_fusion.5
  503.1 1.1 constant_dynamic-slice_fusion.5
  505.1 1.1 constant_dynamic-slice_fusion.5
  507.2 1.1 constant_dynamic-slice_fusion.5
  509.2 1.1 constant_dynamic-slice_fusion.5
  511.2 1.1 constant_dynamic-slice_fusion.5
  513.3 1.1 constant_dynamic-slice_fusion.5
  515.3 1.1 constant_dynamic-slice_fusion.5
  517.4 1.1 constant_dynamic-slice_fusion.5
  519.4 1.1 constant_dynamic-slice_fusion.5
  521.5 1.1 constant_dynamic-slice_fusion.5
  523.5 1.1 constant_dynamic-slice_fusion.5
  525.6 1.1 constant_dynamic-slice_fusion.5
  527.6 1.1 constant_dynamic-slice_fusion.5
  529.7 1.1 constant_dynamic-slice_fusion.5
  531.7 1.1 constant_dynamic-slice_fusion.5
  533.8 1.1 constant_dynamic-slice_fusion.5
  535.8 1.1 constant_dynamic-slice_fusion.5
  537.8 1.1 constant_dynamic-slice_fusion.5
  539.9 1.1 constant_dynamic-slice_fusion.5
  541.9 1.1 constant_dynamic-slice_fusion.5
  544.0 1.1 constant_dynamic-slice_fusion.5
  546.0 1.1 constant_dynamic-slice_fusion.5
  548.1 1.1 constant_dynamic-slice_fusion.5
  550.6 1.3 copy.21
  (121 shorter events, 34.0 us)
Async XLA Ops:
  6.5 23.0 %copy-start = (bf16[2,64,1280]{2,1,0:T(8,128)(2,1)S(1)}, bf16[2,64,1280]{2,1,0:T(8,128)(2,1)}, u32[]{:S(2)}) copy-start(bf16[2,64,1280]{2,1,0:T(8,128)(2,1)} %param.14) | copy-start | bytes 983044
  6.5 22.0 %copy-start.3 = (f32[2,32]{1,0:T(2,128)S(1)}, f32[2,32]{1,0:T(2,128)}, u32[]{:S(2)}) copy-start(f32[2,32]{1,0:T(2,128)} %param.17) | copy-start | bytes 772
  6.5 87.8 %all-reduce.4.cloned.1.call-start = ((), (), s32[]{:S(2)}) async-start(), calls=%async_computation | async-start | bytes 131072 | tf_op jit(solution)/shard_map/psum | solution.py:113
  6.5 11.2 %collective-permute-start = (f32[2,32,2,640]{3,2,1,0:T(2,128)}, f32[2,32,2,640]{3,2,1,0:T(2,128)S(1)}, u32[]{:S(2)}, u32[]{:S(2)}) collective-permute-start(f32[2,32,2,640]{3,2,1,0:T(2,128)} %param.12), channel_id=1, source_target_pairs={{0,8},{8,16},{16,24},{24,32},{32,40},{40,48},{48,56},{56,64},{64,7... | collective-permute-start | bytes 983048 | tf_op jit(solution)/shard_map/ppermute | solution.py:36
  11.1 10.7 %collective-permute-start.1 = (f32[2,32,2,640]{3,2,1,0:T(2,128)}, f32[2,32,2,640]{3,2,1,0:T(2,128)S(1)}, u32[]{:S(2)}, u32[]{:S(2)}) collective-permute-start(f32[2,32,2,640]{3,2,1,0:T(2,128)} %param.12), channel_id=1, source_target_pairs={{8,0},{16,8},{24,16},{32,24},{40,32},{48,40},{56,48},{64,56},{72,6... | collective-permute-start | bytes 983048 | tf_op jit(solution)/shard_map/ppermute | solution.py:38
  17.8 12.0 %copy-start.5 = (s32[2,64]{1,0:T(2,128)S(1)}, s32[2,64]{1,0:T(2,128)}, u32[]{:S(2)}) copy-start(s32[2,64]{1,0:T(2,128)} %param.15) | copy-start | bytes 1540
  17.8 13.0 %copy-start.1 = (f32[2,32,2,640]{3,2,1,0:T(2,128)S(1)}, f32[2,32,2,640]{3,2,1,0:T(2,128)}, u32[]{:S(2)}) copy-start(f32[2,32,2,640]{3,2,1,0:T(2,128)} %param.12) | copy-start | bytes 983044
  19.8 74.6 %copy-start.6 = (f32[2,256]{1,0:T(2,128)S(1)}, f32[2,256]{1,0:T(2,128)}, u32[]{:S(2)}) copy-start(f32[2,256]{1,0:T(2,128)} %param.16) | copy-start | bytes 6148
  21.9 76.3 %collective-permute-start.3 = (f32[6,32,2,640]{3,2,1,0:T(2,128)S(1)}, f32[6,32,2,640]{3,2,1,0:T(2,128)S(1)}, u32[]{:S(2)}, u32[]{:S(2)}) collective-permute-start(f32[6,32,2,640]{3,2,1,0:T(2,128)S(1)} %constant_dynamic-update-slice_fusion), channel_id=1, source_target_pairs={{1,0},{2,1},{3,2},{4,3},{5,4},{6,5},{7,6},{9,8},{10,9},{11,10},{12... | collective-permute-start | bytes 2949128 | tf_op jit(solution)/shard_map/ppermute | solution.py:38
  25.5 72.8 %collective-permute-start.2 = (f32[6,32,2,640]{3,2,1,0:T(2,128)S(1)}, f32[6,32,2,640]{3,2,1,0:T(2,128)}, u32[]{:S(2)}, u32[]{:S(2)}) collective-permute-start(f32[6,32,2,640]{3,2,1,0:T(2,128)S(1)} %constant_dynamic-update-slice_fusion), channel_id=1, source_target_pairs={{0,1},{1,2},{2,3},{3,4},{4,5},{5,6},{6,7},{8,9},{9,10},{10,11},{11... | collective-permute-start | bytes 2949128 | tf_op jit(solution)/shard_map/ppermute | solution.py:36
  29.5 68.7 %copy-start.4 = (f32[2,2,640]{2,1,0:T(2,128)S(1)}, f32[2,2,640]{2,1,0:T(2,128)}, u32[]{:S(2)}) copy-start(f32[2,2,640]{2,1,0:T(2,128)} %param.13) | copy-start | bytes 30724
  30.7 234.5 %all-gather.4.cloned.1.call-start = ((), (), s32[]{:S(2)}) async-start(), calls=%async_computation.1 | async-start | bytes 21626880 | tf_op jit(solution)/shard_map/all_gather | solution.py:16
  98.2 3.2 copy-start.2
  98.2 3.2 copy-start.7
  101.7 1.2 copy-start.9
  102.7 383.8 %all-gather.6.cloned.1.call-start = ((), (), s32[]{:S(2)}) async-start(), calls=%async_computation.2 | async-start | bytes 21626880 | tf_op jit(solution)/shard_map/all_gather | solution.py:16
  265.6 1.2 copy-start.8
Sparse Core Ops, SparseCore 0:
  30.8 63.5 all-reduce.3
  102.8 162.2 all-gather.3
  268.1 218.3 all-gather.5
where the time goes:
time: 560 us; the launch traced here: 558 us
  waiting for transfers between devices  389 us (69%)
  blocking collectives  61.3 us (11%)
  local copies, waits for them, and re-layouts  42.2 us (8%)
  other arithmetic  35.2 us (6%)
  between operations  14.1 us (3%)
  starting transfers between devices  12.5 us (2%)
    all_gather x2, waiting for transfers between devices, carried_in(): gathered = jax.tree.map(lambda a: lax.all_gather(a, axis), part)  319 us
    psum x1, waiting for transfers between devices, shards(): coef = lax.psum(partial_coef, 'xs')  62.9 us
    unnamed x1, blocking collectives  61.3 us
    dynamic_slice x31, local copies, waits for them, and re-layouts, one(): lax.dynamic_index_in_dim(a, source, 0, False)  35.2 us
    add x31, other arithmetic, combine(): later[0][:, None, None] * earlier[1] + later[1]  26.7 us
  transfers between devices with their start and end apart: 7, of which 5 were waited for; matrix products, arithmetic and copies ran while one was open for 2% of the time, Pallas kernels for 0%

commit v1 on v0

--- a/solution.py
+++ b/solution.py
@@ -110,7 +110,8 @@
         jnp.float32
     )
     partial_coef = jnp.einsum("lsq,lsc->lqc", onehot, slot_coef, precision=lax.Precision.HIGHEST)
-    coef = lax.psum(partial_coef, "xs")
+    parts = lax.all_gather(partial_coef, "xs")
+    coef = jnp.sum(parts, axis=0)
     scaled = (strength[:, :, None] * coef).astype(jnp.bfloat16)
     slot_back = jnp.einsum(
         "lsq,lqc->lsc", onehot.astype(jnp.bfloat16), scaled, preferred_element_type=jnp.float32

time: 560 us -> 515 us (0.920)
  waiting for transfers between devices: 389 us -> 324 us
  blocking collectives: 61.3 us -> 78.8 us
    psum x1 -> x0, waiting for transfers between devices: 62.9 us -> none  [shards(): coef = lax.psum(partial_coef, 'xs')]
    all_gather x0 -> x1, blocking collectives: none -> 16.3 us  [shards(): parts = lax.all_gather(partial_coef, 'xs')]
  transfers between devices with their start and end apart: 7 -> 6, of which waited for: 5 -> 4; matrix products, arithmetic and copies ran while one was open for 2% -> 2% of each run, Pallas kernels for 0% -> 0%
where the time goes in v1:
time: 515 us; the launch traced here: 513 us
  waiting for transfers between devices  324 us (63%)
  blocking collectives  78.8 us (15%)
  local copies, waits for them, and re-layouts  43.4 us (8%)
  other arithmetic  36.4 us (7%)
  between operations  14.2 us (3%)
  starting transfers between devices  12.5 us (2%)
    all_gather x2, waiting for transfers between devices, carried_in(): gathered = jax.tree.map(lambda a: lax.all_gather(a, axis), part)  318 us
    unnamed x1, blocking collectives  62.5 us
    dynamic_slice x31, local copies, waits for them, and re-layouts, one(): lax.dynamic_index_in_dim(a, source, 0, False)  35.2 us
    add x31, other arithmetic, combine(): later[0][:, None, None] * earlier[1] + later[1]  26.7 us
    all_gather x1, blocking collectives, shards(): parts = lax.all_gather(partial_coef, 'xs')  16.3 us
  transfers between devices with their start and end apart: 6, of which 4 were waited for; matrix products, arithmetic and copies ran while one was open for 2% of the time, Pallas kernels for 0%

profile of v1, /device:TPU:1, one launch (start us, length us, event | category | flops | bytes accessed | tf_op | source)
XLA Modules:
  0.0 513.0 jit_solution(17840394112578787337)
XLA Ops:
  6.5 4.5 collective-permute-start
  11.1 1.3 collective-permute-start.1
  12.4 1.2 broadcast_multiply_fusion.1
  13.6 4.1 collective-permute-done
  17.8 2.0 constant_dynamic-update-slice_fusion.1
  19.8 2.0 collective-permute-done.1
  21.9 3.6 collective-permute-start.3
  25.5 3.0 collective-permute-start.2
  31.3 16.3 %all-gather = f32[16,256,32]{1,2,0:T(8,128)S(1)} all-gather(f32[2,256,32]{1,2,0:T(8,128)S(1)} %fusion.21), channel_id=2, replica_groups=mesh['layer'=32,'xs'=8] {'xs'}, dimensions={0}, use_global_device_ids=true | all-gather | bytes 589824 | tf_op jit(solution)/shard_map/all_gather | solution.py:113
  47.7 1.8 fusion.2
  49.5 1.9 reshape.101
  51.4 3.2 add_add_fusion
  57.8 62.5 %all-reduce.1 = f32[1024]{0:T(1024)S(1)} all-reduce(f32[1024]{0:T(1024)S(1)} %dynamic-update-slice), channel_id=3, replica_groups=mesh['layer'=32,'xs'=8] {'layer'}, use_global_device_ids=true, to_apply=%add.1 | all-reduce | flops 1024 | bytes 8192
  120.6 98.5 %all-gather.5.cloned.1.call-done = f32[32,4,32,2,640]{4,2,3,1,0:T(8,128)} async-done(((f32[1,4,32,2,640]{4,2,3,1,0:T(8,128)}), f32[32,4,32,2,640]{4,2,3,1,0:T(8,128)}) %all-gather.5.cloned.1.call-update) | async-done | bytes 20971536 | tf_op jit(solution)/shard_map/all_gather | solution.py:16
  221.2 219.5 %all-gather.7.cloned.1.call-done = f32[32,4,32,2,640]{4,2,3,1,0:T(8,128)} async-done(((f32[1,4,32,2,640]{4,2,3,1,0:T(8,128)}), f32[32,4,32,2,640]{4,2,3,1,0:T(8,128)}) %all-gather.7.cloned.1.call-update) | async-done | bytes 20971536 | tf_op jit(solution)/shard_map/all_gather | solution.py:16
  440.9 63.4 %while.27 = (s32[]{:T(128)}, f32[4,32,2,640]{3,2,1,0:T(2,128)S(1)}, s32[]{:T(128)}, f32[32,32]{1,0:T(8,128)S(1)}, f32[32,4,32,2,640]{4,2,3,1,0:T(8,128)}, /*index=5*/s32[]{:T(128)}, s32[]{:T(128)}, s32[]{:T(128)}, s32[]{:T(128)}) while((s32[]{:T(128)}, f32[4,32,2,640]{3,2,1,0:T(2,128)S(1)}, s32[]{:T(128)}, f32[32,32]{1,0:T(8,128)S(1)}, ...), condition=%wide.region_7.8_spmd, body=%wide.region_6.7_spmd.sunk | while | flops 327686 | bytes 3277339 | solution.py:25
  440.9 1.1 constant_dynamic-slice_fusion.5
  443.0 1.1 constant_dynamic-slice_fusion.5
  445.0 1.1 constant_dynamic-slice_fusion.5
  447.1 1.1 constant_dynamic-slice_fusion.5
  449.1 1.1 constant_dynamic-slice_fusion.5
  451.2 1.1 constant_dynamic-slice_fusion.5
  453.2 1.1 constant_dynamic-slice_fusion.5
  455.3 1.1 constant_dynamic-slice_fusion.5
  457.3 1.1 constant_dynamic-slice_fusion.5
  459.4 1.1 constant_dynamic-slice_fusion.5
  461.4 1.1 constant_dynamic-slice_fusion.5
  463.4 1.1 constant_dynamic-slice_fusion.5
  465.5 1.1 constant_dynamic-slice_fusion.5
  467.5 1.1 constant_dynamic-slice_fusion.5
  469.6 1.1 constant_dynamic-slice_fusion.5
  471.6 1.1 constant_dynamic-slice_fusion.5
  473.7 1.1 constant_dynamic-slice_fusion.5
  475.7 1.1 constant_dynamic-slice_fusion.5
  477.8 1.1 constant_dynamic-slice_fusion.5
  479.8 1.1 constant_dynamic-slice_fusion.5
  481.9 1.1 constant_dynamic-slice_fusion.5
  483.9 1.1 constant_dynamic-slice_fusion.5
  485.9 1.1 constant_dynamic-slice_fusion.5
  488.0 1.1 constant_dynamic-slice_fusion.5
  490.0 1.1 constant_dynamic-slice_fusion.5
  492.1 1.1 constant_dynamic-slice_fusion.5
  494.1 1.1 constant_dynamic-slice_fusion.5
  496.2 1.1 constant_dynamic-slice_fusion.5
  498.2 1.1 constant_dynamic-slice_fusion.5
  500.3 1.1 constant_dynamic-slice_fusion.5
  502.3 1.1 constant_dynamic-slice_fusion.5
  504.8 1.3 copy.21
  (126 shorter events, 35.6 us)
Async XLA Ops:
  6.5 24.3 %copy-start = (bf16[2,64,1280]{2,1,0:T(8,128)(2,1)S(1)}, bf16[2,64,1280]{2,1,0:T(8,128)(2,1)}, u32[]{:S(2)}) copy-start(bf16[2,64,1280]{2,1,0:T(8,128)(2,1)} %param.14) | copy-start | bytes 983044
  6.5 22.6 %copy-start.1 = (f32[2,32,2,640]{3,2,1,0:T(2,128)S(1)}, f32[2,32,2,640]{3,2,1,0:T(2,128)}, u32[]{:S(2)}) copy-start(f32[2,32,2,640]{3,2,1,0:T(2,128)} %param.12) | copy-start | bytes 983044
  6.5 22.0 %copy-start.5 = (f32[2,32]{1,0:T(2,128)S(1)}, f32[2,32]{1,0:T(2,128)}, u32[]{:S(2)}) copy-start(f32[2,32]{1,0:T(2,128)} %param.17) | copy-start | bytes 772
  6.5 212.5 %all-gather.5.cloned.1.call-start = ((), (), s32[]{:S(2)}) async-start(), calls=%async_computation | async-start | bytes 21626880 | tf_op jit(solution)/shard_map/all_gather | solution.py:16
  6.5 11.2 %collective-permute-start = (f32[2,32,2,640]{3,2,1,0:T(2,128)}, f32[2,32,2,640]{3,2,1,0:T(2,128)S(1)}, u32[]{:S(2)}, u32[]{:S(2)}) collective-permute-start(f32[2,32,2,640]{3,2,1,0:T(2,128)} %param.12), channel_id=1, source_target_pairs={{0,8},{8,16},{16,24},{24,32},{32,40},{40,48},{48,56},{56,64},{64,7... | collective-permute-start | bytes 983048 | tf_op jit(solution)/shard_map/ppermute | solution.py:36
  11.1 10.7 %collective-permute-start.1 = (f32[2,32,2,640]{3,2,1,0:T(2,128)}, f32[2,32,2,640]{3,2,1,0:T(2,128)S(1)}, u32[]{:S(2)}, u32[]{:S(2)}) collective-permute-start(f32[2,32,2,640]{3,2,1,0:T(2,128)} %param.12), channel_id=1, source_target_pairs={{8,0},{16,8},{24,16},{32,24},{40,32},{48,40},{56,48},{64,56},{72,6... | collective-permute-start | bytes 983048 | tf_op jit(solution)/shard_map/ppermute | solution.py:38
  17.8 13.3 %copy-start.9 = (s32[2,64]{1,0:T(2,128)S(1)}, s32[2,64]{1,0:T(2,128)}, u32[]{:S(2)}) copy-start(s32[2,64]{1,0:T(2,128)} %param.15) | copy-start | bytes 1540
  21.8 9.3 %copy-start.2 = (f32[2,32,2,640]{3,2,1,0:T(2,128)}, f32[2,32,2,640]{3,2,1,0:T(2,128)S(1)}, u32[]{:S(2)}) copy-start(f32[2,32,2,640]{3,2,1,0:T(2,128)S(1)} %collective-permute-done.1) | copy-start | bytes 983044
  21.9 29.5 %collective-permute-start.3 = (f32[6,32,2,640]{3,2,1,0:T(2,128)S(1)}, f32[6,32,2,640]{3,2,1,0:T(2,128)S(1)}, u32[]{:S(2)}, u32[]{:S(2)}) collective-permute-start(f32[6,32,2,640]{3,2,1,0:T(2,128)S(1)} %constant_dynamic-update-slice_fusion), channel_id=1, source_target_pairs={{1,0},{2,1},{3,2},{4,3},{5,4},{6,5},{7,6},{9,8},{10,9},{11,10},{12... | collective-permute-start | bytes 2949128 | tf_op jit(solution)/shard_map/ppermute | solution.py:38
  25.5 25.9 %collective-permute-start.2 = (f32[6,32,2,640]{3,2,1,0:T(2,128)S(1)}, f32[6,32,2,640]{3,2,1,0:T(2,128)}, u32[]{:S(2)}, u32[]{:S(2)}) collective-permute-start(f32[6,32,2,640]{3,2,1,0:T(2,128)S(1)} %constant_dynamic-update-slice_fusion), channel_id=1, source_target_pairs={{0,1},{1,2},{2,3},{3,4},{4,5},{5,6},{6,7},{8,9},{9,10},{10,11},{11... | collective-permute-start | bytes 2949128 | tf_op jit(solution)/shard_map/ppermute | solution.py:36
  47.6 3.8 copy-start.3
  51.4 3.3 copy-start.4
  51.4 3.3 copy-start.10
  54.6 0.6 copy-start.7
  54.6 0.7 copy-start.8
  55.3 1.2 copy-start.12
  56.3 384.4 %all-gather.7.cloned.1.call-start = ((), (), s32[]{:S(2)}) async-start(), calls=%async_computation.1 | async-start | bytes 21626880 | tf_op jit(solution)/shard_map/all_gather | solution.py:16
  219.3 0.6 copy-start.6
  219.9 1.1 copy-start.11
Sparse Core Ops, SparseCore 0:
  56.4 162.5 all-gather.4
  221.6 219.0 all-gather.6
